TPU v7x, 32 devices: a whole 2x2x4 slice. The times are simulated.
32 devices in a mesh: leaf: 32 (over z, y, x, core).
Axes of the slice: x: 2, y: 2, z: 4, core: 2. Of those that a mesh axis runs over, the one named last changes fastest.
Arguments:
- near_blocks: bfloat16 [64, 26, 256, 256], P('leaf'), may hold values from -0.0582 to 0.0582
- diag_blocks: bfloat16 [64, 256, 256], P('leaf'), as said below
- bases: bfloat16 [64, 256, 256], P('leaf'), as said below
- leaf_nbrs: int32 [64, 26], P('leaf'), may hold values from -1 to 63, as said below
- parent_nbrs: int32 [8, 5], replicated, may hold values from 0 to 7, as said below
Outputs:
- leaf_factor: float32 [64, 128, 128], P('leaf')
- leaf_panel: float32 [64, 128, 128], P('leaf')
- merged: float32 [64, 5, 128, 1024], P('leaf')
- parent_block: float32 [8192, 1024], P('leaf')
Inputs may be any that keep to these rules, and one draw needn't show every extreme that they name: `leaf_nbrs`: row i lists distinct leaves j with j != i and |j - i| <= 16; live entries come first and -1 fills the rest; every row has at least 13 live entries and some row has all 26. `parent_nbrs`: row P begins with P itself, followed by the other 4 parents nearest to P in numbering, distinct, equally near ones in any order. `diag_blocks`: each block is symmetric positive definite. `bases`: each basis is an orthogonal matrix rounded to bfloat16.
All inputs are finite; a program needn't handle non-finite values.
Results may differ from a plain program's by a relative error of at most 0.001.
The roundings to bfloat16 on the way count: a program that leaves them out, or rounds other values in their place, can miss the bound.
Values may be sent and summed in bfloat16 or wider, within the bound.
A program may use at most 128 MiB of HBM per device.

v0:
```python
import jax
import jax.numpy as jnp
from jax import lax
from jax.sharding import PartitionSpec as P

RANK = 128
REACH = 16
CHILDREN = 8


highest = lax.Precision.HIGHEST


def shortened(value):

    def short(part):
        return part.astype(jnp.bfloat16) if part.dtype == jnp.float32 else part

    return jax.tree.map(short, value)


def passed_along(value, axis, steps):
    count = lax.axis_size(axis)
    leading, last = (max(0, -steps), min(count, count - steps))
    return lax.ppermute(value, axis, [(source, source + steps) for source in range(leading, last)])


def partner_2(value, axis, apart):
    mask = 2**apart
    pairs = [(source, source ^ mask) for source in range(lax.axis_size(axis))]
    return lax.ppermute(value, axis, pairs)


def lower_solve(lower_factor, right_side):
    return lax.linalg.triangular_solve(lower_factor, right_side, left_side=True, lower=True)


def back_solve(lower_factor, right_side):
    return lax.linalg.triangular_solve(
        lower_factor, right_side, left_side=True, lower=True, transpose_a=True
    )


def flatten_front(tensor):
    return tensor.reshape((tensor.shape[0] * tensor.shape[1],) + tensor.shape[2:])


def join_front(head_part, tail_part):
    return jnp.concatenate([head_part, tail_part])


def local(near_blocks, diag_blocks, bases, leaf_nbrs, parent_nbrs):
    per_device = bases.shape[0]
    leaf_rows = bases.shape[1]
    redundant = leaf_rows - RANK
    device = lax.axis_index("leaf")
    span_dev = REACH // per_device
    half_diag = jnp.einsum(
        "lba,lbc->lac", bases, diag_blocks, preferred_element_type=jnp.float32
    ).astype(jnp.bfloat16)
    dense_diag = jnp.einsum("lac,lcb->lab", half_diag, bases, preferred_element_type=jnp.float32)
    leaf_factor = jnp.linalg.cholesky(dense_diag[:, :redundant, :redundant])
    leaf_panel = lower_solve(leaf_factor, dense_diag[:, :redundant, redundant:])
    skeleton = dense_diag[:, redundant:, redundant:] - jnp.einsum(
        "lka,lkb->lab", leaf_panel, leaf_panel, precision=highest
    )
    leaf_shift = lax.optimization_barrier(back_solve(leaf_factor, leaf_panel).astype(jnp.bfloat16))
    package = (bases, leaf_shift)
    half_proj = jnp.einsum(
        "lba,lnbc->lnac", bases, near_blocks, preferred_element_type=jnp.float32
    ).astype(jnp.bfloat16)
    lower_side = jax.tree.map(lambda tensor: tensor[None], package)
    upper_side = lower_side
    covered = 0
    while covered < span_dev:
        stride = covered + 1
        amount = min(stride, span_dev - covered)
        outgoing_low = jax.tree.map(lambda tensor: tensor[:amount], lower_side)
        outgoing_high = jax.tree.map(lambda tensor: tensor[:amount], upper_side)
        incoming_low = jax.tree.map(
            lambda part, own: part.astype(own.dtype),
            passed_along(shortened(outgoing_low), "leaf", stride),
            outgoing_low,
        )
        incoming_high = jax.tree.map(
            lambda part, own: part.astype(own.dtype),
            passed_along(shortened(outgoing_high), "leaf", -stride),
            outgoing_high,
        )
        lower_side = jax.tree.map(join_front, lower_side, incoming_low)
        upper_side = jax.tree.map(join_front, upper_side, incoming_high)
        covered = covered + amount
    window = jax.tree.map(
        lambda head_part, tail_part: jnp.concatenate([head_part[::-1], tail_part[1:]]),
        lower_side,
        upper_side,
    )
    win_bases, win_shift = jax.tree.map(flatten_front, window)
    leaf_ids = device * per_device + jnp.arange(per_device, dtype=jnp.int32)
    is_live = leaf_nbrs >= 0
    clipped = jnp.maximum(leaf_nbrs, 0)
    window_slot = (clipped // per_device - device + span_dev) * per_device + clipped % per_device
    window_slot = jnp.clip(window_slot, 0, (2 * span_dev + 1) * per_device - 1)
    near_bases = win_bases[window_slot]
    near_shift = win_shift[window_slot].astype(jnp.float32)
    own_shift = leaf_shift.astype(jnp.float32)
    coupled = jnp.einsum(
        "lnac,lncb->lnab", half_proj, near_bases, preferred_element_type=jnp.float32
    )
    first_term = jnp.einsum(
        "lka,lnkb->lnab", own_shift, coupled[:, :, :redundant, redundant:], precision=highest
    )
    second_term = jnp.einsum(
        "lnak,lnkb->lnab", coupled[:, :, redundant:, :redundant], near_shift, precision=highest
    )
    near_schur = jnp.where(
        is_live[:, :, None, None],
        coupled[:, :, redundant:, redundant:] - first_term - second_term,
        jnp.float32(0.0),
    )
    children = jnp.arange(CHILDREN, dtype=jnp.int32)
    parent = leaf_ids // CHILDREN
    position = leaf_ids % CHILDREN
    parent_count = parent_nbrs.shape[0]
    selector = (jnp.arange(parent_count, dtype=jnp.int32)[None, :] == parent[:, None]).astype(
        jnp.int32
    )
    targets = jnp.sum(selector[:, :, None] * parent_nbrs[None, :, :], axis=1)
    slot_hits = (
        is_live[:, None, None, :]
        & (clipped[:, None, None, :] // CHILDREN == targets[:, :, None, None])
        & (clipped[:, None, None, :] % CHILDREN == children[None, None, :, None])
    )
    self_hit = (targets[:, :, None] == parent[:, None, None]) & (
        children[None, None, :] == position[:, None, None]
    )
    parent_rows = jnp.einsum(
        "lqbn,lnxy->lqxby", slot_hits.astype(jnp.float32), near_schur, precision=highest
    )
    parent_rows = (
        parent_rows
        + self_hit.astype(jnp.float32)[:, :, None, :, None] * skeleton[:, None, :, None, :]
    )
    merged = parent_rows.reshape(parent_rows.shape[0], parent_rows.shape[1], RANK, CHILDREN * RANK)
    own_rows = merged[:, 0].reshape(per_device * RANK, CHILDREN * RANK)
    group_size = CHILDREN // per_device
    group_place = device % group_size
    gathered = own_rows
    for bit_number in range(group_size.bit_length() - 1):
        partner = partner_2(gathered.astype(jnp.bfloat16), "leaf", bit_number).astype(
            gathered.dtype
        )
        is_upper = device // (1 << bit_number) % 2 == 1
        gathered = jnp.where(
            is_upper, jnp.concatenate([partner, gathered]), jnp.concatenate([gathered, partner])
        )
    own_columns = lax.dynamic_slice_in_dim(
        gathered, group_place * per_device * RANK, per_device * RANK, 1
    )
    parent_block = 0.5 * (own_rows + own_columns.T)
    return (leaf_factor, leaf_panel, merged, parent_block)


def solution(mesh):
    in_specs = (
        P("leaf", None, None, None),
        P("leaf", None, None),
        P("leaf", None, None),
        P("leaf", None),
        P(),
    )
    out_specs = (
        P("leaf", None, None),
        P("leaf", None, None),
        P("leaf", None, None, None),
        P("leaf", None),
    )
    return jax.shard_map(local, mesh=mesh, in_specs=in_specs, out_specs=out_specs, check_vma=False)
```

profile of v0, /device:TPU:23, one launch (start us, length us, event | category | flops | bytes accessed | tf_op | source)
XLA Modules:
  0.0 250.9 jit_solution(6261922632020300109)
XLA Ops:
  0.7 3.8 %collective-permute-start = (bf16[1,2,256,256]{3,2,1,0:T(8,128)(2,1)}, bf16[1,2,256,256]{3,2,1,0:T(8,128)(2,1)S(1)}, u32[]{:S(2)}, u32[]{:S(2)}) collective-permute-start(bf16[1,2,256,256]{3,2,1,0:T(8,128)(2,1)} %bitcast.62), channel_id=1, source_target_pairs={{0,1},{1,2},{2,3},{3,4},{4,5},{5,6},{6,7},{7,8},{8,9},{9,10},{10,1... | collective-permute-start | bytes 786440 | tf_op jit(solution)/shard_map/ppermute | solution.py:25
  10.2 23.5 %custom-call.9 = f32[2,128,128]{2,1,0:T(8,128)S(1)} custom-call(f32[2,128,128]{2,1,0:T(8,128)S(1)} %fusion.34), custom_call_target="Cholesky" | custom-call | tf_op jit(solution)/shard_map/jit(cholesky)/cholesky | solution.py:62
  34.6 19.7 %custom-call.10 = f32[2,1,128,128]{2,3,1,0:T(8,128)S(1)} custom-call(f32[2,1,128,128]{3,2,1,0:T(8,128)S(1)} %get-tuple-element.22), custom_call_target="InvertDiagBlocksLowerTriangular" | custom-call | tf_op jit(solution)/shard_map/triangular_solve | solution.py:35
  54.9 4.6 %collective-permute-start.8 = (bf16[1,2,128,128]{3,2,1,0:T(8,128)(2,1)S(1)}, bf16[1,2,128,128]{3,2,1,0:T(8,128)(2,1)S(1)}, u32[]{:S(2)}, u32[]{:S(2)}) collective-permute-start(bf16[1,2,128,128]{3,2,1,0:T(8,128)(2,1)S(1)} %bitcast.71), channel_id=1, source_target_pairs={{0,1},{1,2},{2,3},{3,4},{4,5},{5,6},{6,7},{7,8},{8,9},{9,10},{10,1... | collective-permute-start | bytes 196616 | tf_op jit(solution)/shard_map/ppermute | solution.py:25
  66.9 3.3 %collective-permute-start.5 = (bf16[2,2,256,256]{3,2,1,0:T(8,128)(2,1)S(1)}, bf16[2,2,256,256]{3,2,1,0:T(8,128)(2,1)S(1)}, u32[]{:S(2)}, u32[]{:S(2)}) collective-permute-start(bf16[2,2,256,256]{3,2,1,0:T(8,128)(2,1)S(1)} %get-tuple-element.26), channel_id=1, source_target_pairs={{2,0},{3,1},{4,2},{5,3},{6,4},{7,5},{8,6},{9,7},{10,8},{11,9},{12,... | collective-permute-start | bytes 1572872 | tf_op jit(solution)/shard_map/ppermute | solution.py:25
  70.2 3.8 %collective-permute-start.9 = (bf16[2,2,128,128]{3,2,1,0:T(8,128)(2,1)S(1)}, bf16[2,2,128,128]{3,2,1,0:T(8,128)(2,1)S(1)}, u32[]{:S(2)}, u32[]{:S(2)}) collective-permute-start(bf16[2,2,128,128]{3,2,1,0:T(8,128)(2,1)S(1)} %get-tuple-element.31), channel_id=1, source_target_pairs={{0,2},{1,3},{2,4},{3,5},{4,6},{5,7},{6,8},{7,9},{8,10},{9,11},{10,... | collective-permute-start | bytes 393224 | tf_op jit(solution)/shard_map/ppermute | solution.py:25
  76.0 16.6 %collective-permute-done.9 = bf16[2,2,128,128]{3,2,1,0:T(8,128)(2,1)S(1)} collective-permute-done((bf16[2,2,128,128]{3,2,1,0:T(8,128)(2,1)S(1)}, bf16[2,2,128,128]{3,2,1,0:T(8,128)(2,1)S(1)}, u32[]{:S(2)}, u32[]{:S(2)}) %collective-permute-start.9) | collective-permute-done | bytes 131104 | tf_op jit(solution)/shard_map/ppermute | solution.py:25
  92.6 6.1 %collective-permute-start.7 = (bf16[1,2,256,256]{3,2,1,0:T(8,128)(2,1)S(1)}, bf16[1,2,256,256]{3,2,1,0:T(8,128)(2,1)}, u32[]{:S(2)}, u32[]{:S(2)}) collective-permute-start(bf16[1,2,256,256]{3,2,1,0:T(8,128)(2,1)S(1)} %bitcast.66), channel_id=1, source_target_pairs={{8,0},{9,1},{10,2},{11,3},{12,4},{13,5},{14,6},{15,7},{16,8},{17,9... | collective-permute-start | bytes 786440 | tf_op jit(solution)/shard_map/ppermute | solution.py:25
  100.7 3.1 %collective-permute-start.10 = (bf16[4,2,128,128]{3,2,1,0:T(8,128)(2,1)S(1)}, bf16[4,2,128,128]{3,2,1,0:T(8,128)(2,1)S(1)}, u32[]{:S(2)}, u32[]{:S(2)}) collective-permute-start(bf16[4,2,128,128]{3,2,1,0:T(8,128)(2,1)S(1)} %get-tuple-element.29), channel_id=1, source_target_pairs={{0,4},{1,5},{2,6},{3,7},{4,8},{5,9},{6,10},{7,11},{8,12},{9,13},{1... | collective-permute-start | bytes 786440 | tf_op jit(solution)/shard_map/ppermute | solution.py:25
  108.5 4.2 %collective-permute-start.14 = (bf16[4,2,128,128]{3,2,1,0:T(8,128)(2,1)S(1)}, bf16[4,2,128,128]{3,2,1,0:T(8,128)(2,1)S(1)}, u32[]{:S(2)}, u32[]{:S(2)}) collective-permute-start(bf16[4,2,128,128]{3,2,1,0:T(8,128)(2,1)S(1)} %get-tuple-element.28), channel_id=1, source_target_pairs={{4,0},{5,1},{6,2},{7,3},{8,4},{9,5},{10,6},{11,7},{12,8},{13,9},{1... | collective-permute-start | bytes 786440 | tf_op jit(solution)/shard_map/ppermute | solution.py:25
  112.9 2.9 %collective-permute-start.6 = (bf16[4,2,256,256]{3,2,1,0:T(8,128)(2,1)}, bf16[4,2,256,256]{3,2,1,0:T(8,128)(2,1)}, u32[]{:S(2)}, u32[]{:S(2)}) collective-permute-start(bf16[4,2,256,256]{3,2,1,0:T(8,128)(2,1)} %get-tuple-element.24), channel_id=1, source_target_pairs={{4,0},{5,1},{6,2},{7,3},{8,4},{9,5},{10,6},{11,7},{12,8},{13,9},{1... | collective-permute-start | bytes 3145736 | tf_op jit(solution)/shard_map/ppermute | solution.py:25
  115.9 24.7 %collective-permute-done.14 = bf16[4,2,128,128]{3,2,1,0:T(8,128)(2,1)S(1)} collective-permute-done((bf16[4,2,128,128]{3,2,1,0:T(8,128)(2,1)S(1)}, bf16[4,2,128,128]{3,2,1,0:T(8,128)(2,1)S(1)}, u32[]{:S(2)}, u32[]{:S(2)}) %collective-permute-start.14) | collective-permute-done | bytes 262176 | tf_op jit(solution)/shard_map/ppermute | solution.py:25
  142.9 3.1 %collective-permute-done.15 = bf16[1,2,128,128]{3,2,1,0:T(8,128)(2,1)S(1)} collective-permute-done((bf16[1,2,128,128]{3,2,1,0:T(8,128)(2,1)S(1)}, bf16[1,2,128,128]{3,2,1,0:T(8,128)(2,1)S(1)}, u32[]{:S(2)}, u32[]{:S(2)}) %collective-permute-start.15) | collective-permute-done | bytes 65568 | tf_op jit(solution)/shard_map/ppermute | solution.py:25
  148.8 12.1 %collective-permute-done.2 = bf16[4,2,256,256]{3,2,1,0:T(8,128)(2,1)} collective-permute-done((bf16[4,2,256,256]{3,2,1,0:T(8,128)(2,1)}, bf16[4,2,256,256]{3,2,1,0:T(8,128)(2,1)}, u32[]{:S(2)}, u32[]{:S(2)}) %collective-permute-start.2) | collective-permute-done | bytes 1048608 | tf_op jit(solution)/shard_map/ppermute | solution.py:25
  164.8 3.3 %reverse_dynamic-update-slice_fusion = bf16[17,2,256,256]{3,2,1,0:T(8,128)(2,1)} fusion(bf16[9,2,256,256]{3,2,1,0:T(8,128)(2,1)} %constant_dynamic-update-slice_fusion), kind=kLoop, calls=%fused_computation.20 | loop fusion | bytes 4718592
  173.6 7.3 %gather_fusion = bf16[52,256,256]{2,1,0:T(8,128)(2,1)} fusion(bf16[34,256,256]{2,1,0:T(8,128)(2,1)} %bitcast.6, s32[1024]{0:T(1024)S(1)} %pad_clamp_fusion), kind=kCustom, calls=%fused_computation | custom fusion | bytes 13631696 | tf_op jit(solution)/shard_map/gather | solution.py:104
  180.9 12.5 %fusion = f32[2,26,256,256]{3,2,1,0:T(8,128)} fusion(bf16[2,26,256,256]{3,2,1,0:T(8,128)(2,1)} %bitcast.59, bf16[2,26,256,256]{3,2,1,0:T(8,128)(2,1)} %param.5, bf16[2,256,256]{2,1,0:T(8,128)(2,1)S(1)} %copy-done.2), kind=kOutput, calls=%fused_computation.2 | convolution fusion | flops 3493068800 | bytes 27525120 | tf_op jit(solution)/shard_map/lnac,lncb->lnab/dot_general | solution.py:107
  193.3 3.9 %fusion.8 = f32[2,26,128,128]{2,3,1,0:T(8,128)S(1)} fusion(f32[2,26,256,256]{3,2,1,0:T(8,128)} %fusion, bf16[2,128,128]{2,1,0:T(8,128)(2,1)S(1)} %convolution_convert_fusion.1), kind=kOutput, calls=%fused_computation.14 | convolution fusion | flops 1308622848 | bytes 6881280 | tf_op jit(solution)/shard_map/lka,lnkb->lnab/dot_general | solution.py:110
  197.3 5.6 %fusion.12 = f32[2,26,128,128,1]{3,2,1,0,4:T(8,128)S(1)} fusion(f32[2,26,256,256]{3,2,1,0:T(8,128)} %fusion, f32[2,26,128,128]{2,3,1,0:T(8,128)S(1)} %fusion.8, bf16[2,26,128,128]{3,2,1,0:T(8,128)(2,1)S(1)} %bitcast.69, pred[2,26]{1,0:T(4,128)(4,1)S(1)} %copy-done.13), kind=kOutput, calls=%fused_computation.19 | convolution fusion | flops 1311178752 | bytes 15335476 | tf_op jit(solution)/shard_map/lnak,lnkb->lnab/dot_general | solution.py:113
  203.0 7.8 %bitcast_add_fusion = f32[2,5,128,8,128]{4,3,1,2,0:T(8,128)} fusion(f32[2,128,128]{2,1,0:T(8,128)S(1)} %copy-done.10, f32[2,5,8]{2,1,0:T(8,128)S(1)} %and_convert_fusion, f32[2,26,128,128,1]{3,2,1,0,4:T(8,128)S(1)} %fusion.12, pred[2,8,26]{2,1,0:T(8,128)(4,1)S(1)} %copy-done.11, pred[2,5,26]{2,1,0:T(8,128)(4,1)S(1)} %compare_and_fusion), kind=kOutput, calls=%fused_computation.5 | convolution fusion | flops 411568160 | bytes 8782820 | tf_op jit(solution)/shard_map/lqbn,lnxy->lqxby/dot_general | solution.py:137
  210.8 6.3 %copy.54 = f32[2,5,128,8,128]{2,4,3,1,0:T(8,128)} copy(f32[2,5,128,8,128]{4,3,1,2,0:T(8,128)} %bitcast_add_fusion) | data formatting | bytes 10485760 | tf_op jit(solution)/shard_map/add | solution.py:141
  219.1 2.6 %collective-permute-start.16 = (bf16[256,1024]{0,1:T(8,128)(2,1)S(1)}, bf16[256,1024]{0,1:T(8,128)(2,1)S(1)}, u32[]{:S(2)}, u32[]{:S(2)}) collective-permute-start(bf16[256,1024]{0,1:T(8,128)(2,1)S(1)} %convert_element_type.44), channel_id=1, source_target_pairs={{0,1},{1,0},{2,3},{3,2},{4,5},{5,4},{6,7},{7,6},{8,9},{9,8},{10,11... | collective-permute-start | bytes 1572872 | tf_op jit(solution)/shard_map/ppermute | solution.py:31
  225.3 5.9 %copy.59 = f32[2,5,128,1024]{3,2,1,0:T(8,128)} copy(f32[2,5,128,1024]{2,3,1,0:T(8,128)} %bitcast.61) | data formatting | bytes 10485760
  231.2 18.1 %collective-permute-done.17 = bf16[512,1024]{0,1:T(8,128)(2,1)S(1)} collective-permute-done((bf16[512,1024]{0,1:T(8,128)(2,1)S(1)}, bf16[512,1024]{0,1:T(8,128)(2,1)S(1)}, u32[]{:S(2)}, u32[]{:S(2)}) %collective-permute-start.17) | collective-permute-done | bytes 1048608 | tf_op jit(solution)/shard_map/ppermute | solution.py:31
  (113 shorter events, 45.0 us)
Async XLA Ops:
  0.6 60.8 %copy-start.2 = (bf16[2,256,256]{2,1,0:T(8,128)(2,1)S(1)}, bf16[2,256,256]{2,1,0:T(8,128)(2,1)}, u32[]{:S(2)}) copy-start(bf16[2,256,256]{2,1,0:T(8,128)(2,1)} %param.7) | copy-start | bytes 786436
  0.7 61.5 %copy-start.15 = (s32[2,26]{1,0:T(2,128)S(1)}, s32[2,26]{1,0:T(2,128)}, u32[]{:S(2)}) copy-start(s32[2,26]{1,0:T(2,128)} %param.8) | copy-start | bytes 628
  0.7 61.6 %copy-start.14 = (s32[8,5]{1,0:T(8,128)S(1)}, s32[8,5]{1,0:T(8,128)}, u32[]{:S(2)}) copy-start(s32[8,5]{1,0:T(8,128)} %param.9) | copy-start | bytes 484
  0.7 64.0 %collective-permute-start = (bf16[1,2,256,256]{3,2,1,0:T(8,128)(2,1)}, bf16[1,2,256,256]{3,2,1,0:T(8,128)(2,1)S(1)}, u32[]{:S(2)}, u32[]{:S(2)}) collective-permute-start(bf16[1,2,256,256]{3,2,1,0:T(8,128)(2,1)} %bitcast.62), channel_id=1, source_target_pairs={{0,1},{1,2},{2,3},{3,4},{4,5},{5,6},{6,7},{7,8},{8,9},{9,10},{10,1... | collective-permute-start | bytes 786440 | tf_op jit(solution)/shard_map/ppermute | solution.py:25
  4.5 60.2 %collective-permute-start.4 = (bf16[1,2,256,256]{3,2,1,0:T(8,128)(2,1)}, bf16[1,2,256,256]{3,2,1,0:T(8,128)(2,1)S(1)}, u32[]{:S(2)}, u32[]{:S(2)}) collective-permute-start(bf16[1,2,256,256]{3,2,1,0:T(8,128)(2,1)} %bitcast.63), channel_id=1, source_target_pairs={{1,0},{2,1},{3,2},{4,3},{5,4},{6,5},{7,6},{8,7},{9,8},{10,9},{11,1... | collective-permute-start | bytes 786440 | tf_op jit(solution)/shard_map/ppermute | solution.py:25
  6.4 156.7 %collective-permute-start.3 = (bf16[1,2,256,256]{3,2,1,0:T(8,128)(2,1)}, bf16[1,2,256,256]{3,2,1,0:T(8,128)(2,1)}, u32[]{:S(2)}, u32[]{:S(2)}) collective-permute-start(bf16[1,2,256,256]{3,2,1,0:T(8,128)(2,1)} %bitcast.64), channel_id=1, source_target_pairs={{0,8},{1,9},{2,10},{3,11},{4,12},{5,13},{6,14},{7,15},{8,16},{9,17... | collective-permute-start | bytes 786440 | tf_op jit(solution)/shard_map/ppermute | solution.py:25
  54.6 50.8 %copy-start.9 = (f32[2,128,128]{2,1,0:T(8,128)}, f32[2,128,128]{2,1,0:T(8,128)S(1)}, u32[]{:S(2)}) copy-start(f32[2,128,128]{2,1,0:T(8,128)S(1)} %fusion.30) | copy-start | bytes 393220
  54.9 15.2 %collective-permute-start.8 = (bf16[1,2,128,128]{3,2,1,0:T(8,128)(2,1)S(1)}, bf16[1,2,128,128]{3,2,1,0:T(8,128)(2,1)S(1)}, u32[]{:S(2)}, u32[]{:S(2)}) collective-permute-start(bf16[1,2,128,128]{3,2,1,0:T(8,128)(2,1)S(1)} %bitcast.71), channel_id=1, source_target_pairs={{0,1},{1,2},{2,3},{3,4},{4,5},{5,6},{6,7},{7,8},{8,9},{9,10},{10,1... | collective-permute-start | bytes 196616 | tf_op jit(solution)/shard_map/ppermute | solution.py:25
  59.5 10.6 %collective-permute-start.12 = (bf16[1,2,128,128]{3,2,1,0:T(8,128)(2,1)S(1)}, bf16[1,2,128,128]{3,2,1,0:T(8,128)(2,1)S(1)}, u32[]{:S(2)}, u32[]{:S(2)}) collective-permute-start(bf16[1,2,128,128]{3,2,1,0:T(8,128)(2,1)S(1)} %bitcast.72), channel_id=1, source_target_pairs={{1,0},{2,1},{3,2},{4,3},{5,4},{6,5},{7,6},{8,7},{9,8},{10,9},{11,1... | collective-permute-start | bytes 196616 | tf_op jit(solution)/shard_map/ppermute | solution.py:25
  64.7 40.6 %copy-start.4 = (bf16[1,2,256,256]{3,2,1,0:T(8,128)(2,1)}, bf16[1,2,256,256]{3,2,1,0:T(8,128)(2,1)S(1)}, u32[]{:S(2)}) copy-start(bf16[1,2,256,256]{3,2,1,0:T(8,128)(2,1)S(1)} %collective-permute-done.4) | copy-start | bytes 786436
  64.8 35.9 %collective-permute-start.1 = (bf16[2,2,256,256]{3,2,1,0:T(8,128)(2,1)S(1)}, bf16[2,2,256,256]{3,2,1,0:T(8,128)(2,1)S(1)}, u32[]{:S(2)}, u32[]{:S(2)}) collective-permute-start(bf16[2,2,256,256]{3,2,1,0:T(8,128)(2,1)S(1)} %get-tuple-element.27), channel_id=1, source_target_pairs={{0,2},{1,3},{2,4},{3,5},{4,6},{5,7},{6,8},{7,9},{8,10},{9,11},{10,... | collective-permute-start | bytes 1572872 | tf_op jit(solution)/shard_map/ppermute | solution.py:25
  66.9 37.0 %collective-permute-start.5 = (bf16[2,2,256,256]{3,2,1,0:T(8,128)(2,1)S(1)}, bf16[2,2,256,256]{3,2,1,0:T(8,128)(2,1)S(1)}, u32[]{:S(2)}, u32[]{:S(2)}) collective-permute-start(bf16[2,2,256,256]{3,2,1,0:T(8,128)(2,1)S(1)} %get-tuple-element.26), channel_id=1, source_target_pairs={{2,0},{3,1},{4,2},{5,3},{6,4},{7,5},{8,6},{9,7},{10,8},{11,9},{12,... | collective-permute-start | bytes 1572872 | tf_op jit(solution)/shard_map/ppermute | solution.py:25
  70.2 22.4 %collective-permute-start.9 = (bf16[2,2,128,128]{3,2,1,0:T(8,128)(2,1)S(1)}, bf16[2,2,128,128]{3,2,1,0:T(8,128)(2,1)S(1)}, u32[]{:S(2)}, u32[]{:S(2)}) collective-permute-start(bf16[2,2,128,128]{3,2,1,0:T(8,128)(2,1)S(1)} %get-tuple-element.31), channel_id=1, source_target_pairs={{0,2},{1,3},{2,4},{3,5},{4,6},{5,7},{6,8},{7,9},{8,10},{9,11},{10,... | collective-permute-start | bytes 393224 | tf_op jit(solution)/shard_map/ppermute | solution.py:25
  74.0 24.7 %collective-permute-start.13 = (bf16[2,2,128,128]{3,2,1,0:T(8,128)(2,1)S(1)}, bf16[2,2,128,128]{3,2,1,0:T(8,128)(2,1)S(1)}, u32[]{:S(2)}, u32[]{:S(2)}) collective-permute-start(bf16[2,2,128,128]{3,2,1,0:T(8,128)(2,1)S(1)} %get-tuple-element.30), channel_id=1, source_target_pairs={{2,0},{3,1},{4,2},{5,3},{6,4},{7,5},{8,6},{9,7},{10,8},{11,9},{12,... | collective-permute-start | bytes 393224 | tf_op jit(solution)/shard_map/ppermute | solution.py:25
  92.6 79.3 %collective-permute-start.7 = (bf16[1,2,256,256]{3,2,1,0:T(8,128)(2,1)S(1)}, bf16[1,2,256,256]{3,2,1,0:T(8,128)(2,1)}, u32[]{:S(2)}, u32[]{:S(2)}) collective-permute-start(bf16[1,2,256,256]{3,2,1,0:T(8,128)(2,1)S(1)} %bitcast.66), channel_id=1, source_target_pairs={{8,0},{9,1},{10,2},{11,3},{12,4},{13,5},{14,6},{15,7},{16,8},{17,9... | collective-permute-start | bytes 786440 | tf_op jit(solution)/shard_map/ppermute | solution.py:25
  98.7 14.1 %collective-permute-start.11 = (bf16[1,2,128,128]{3,2,1,0:T(8,128)(2,1)S(1)}, bf16[1,2,128,128]{3,2,1,0:T(8,128)(2,1)S(1)}, u32[]{:S(2)}, u32[]{:S(2)}) collective-permute-start(bf16[1,2,128,128]{3,2,1,0:T(8,128)(2,1)S(1)} %bitcast.74), channel_id=1, source_target_pairs={{0,8},{1,9},{2,10},{3,11},{4,12},{5,13},{6,14},{7,15},{8,16},{9,17... | collective-permute-start | bytes 196616 | tf_op jit(solution)/shard_map/ppermute | solution.py:25
  100.7 42.2 %copy-start.8 = (bf16[2,2,256,256]{3,2,1,0:T(8,128)(2,1)}, bf16[2,2,256,256]{3,2,1,0:T(8,128)(2,1)S(1)}, u32[]{:S(2)}) copy-start(bf16[2,2,256,256]{3,2,1,0:T(8,128)(2,1)S(1)} %collective-permute-done.1) | copy-start | bytes 1572868
  100.7 7.8 %collective-permute-start.10 = (bf16[4,2,128,128]{3,2,1,0:T(8,128)(2,1)S(1)}, bf16[4,2,128,128]{3,2,1,0:T(8,128)(2,1)S(1)}, u32[]{:S(2)}, u32[]{:S(2)}) collective-permute-start(bf16[4,2,128,128]{3,2,1,0:T(8,128)(2,1)S(1)} %get-tuple-element.29), channel_id=1, source_target_pairs={{0,4},{1,5},{2,6},{3,7},{4,8},{5,9},{6,10},{7,11},{8,12},{9,13},{1... | collective-permute-start | bytes 786440 | tf_op jit(solution)/shard_map/ppermute | solution.py:25
  105.4 55.5 %collective-permute-start.2 = (bf16[4,2,256,256]{3,2,1,0:T(8,128)(2,1)}, bf16[4,2,256,256]{3,2,1,0:T(8,128)(2,1)}, u32[]{:S(2)}, u32[]{:S(2)}) collective-permute-start(bf16[4,2,256,256]{3,2,1,0:T(8,128)(2,1)} %get-tuple-element.25), channel_id=1, source_target_pairs={{0,4},{1,5},{2,6},{3,7},{4,8},{5,9},{6,10},{7,11},{8,12},{9,13},{1... | collective-permute-start | bytes 3145736 | tf_op jit(solution)/shard_map/ppermute | solution.py:25
  108.5 32.1 %collective-permute-start.14 = (bf16[4,2,128,128]{3,2,1,0:T(8,128)(2,1)S(1)}, bf16[4,2,128,128]{3,2,1,0:T(8,128)(2,1)S(1)}, u32[]{:S(2)}, u32[]{:S(2)}) collective-permute-start(bf16[4,2,128,128]{3,2,1,0:T(8,128)(2,1)S(1)} %get-tuple-element.28), channel_id=1, source_target_pairs={{4,0},{5,1},{6,2},{7,3},{8,4},{9,5},{10,6},{11,7},{12,8},{13,9},{1... | collective-permute-start | bytes 786440 | tf_op jit(solution)/shard_map/ppermute | solution.py:25
  112.9 56.8 %collective-permute-start.6 = (bf16[4,2,256,256]{3,2,1,0:T(8,128)(2,1)}, bf16[4,2,256,256]{3,2,1,0:T(8,128)(2,1)}, u32[]{:S(2)}, u32[]{:S(2)}) collective-permute-start(bf16[4,2,256,256]{3,2,1,0:T(8,128)(2,1)} %get-tuple-element.24), channel_id=1, source_target_pairs={{4,0},{5,1},{6,2},{7,3},{8,4},{9,5},{10,6},{11,7},{12,8},{13,9},{1... | collective-permute-start | bytes 3145736 | tf_op jit(solution)/shard_map/ppermute | solution.py:25
  140.6 5.4 %collective-permute-start.15 = (bf16[1,2,128,128]{3,2,1,0:T(8,128)(2,1)S(1)}, bf16[1,2,128,128]{3,2,1,0:T(8,128)(2,1)S(1)}, u32[]{:S(2)}, u32[]{:S(2)}) collective-permute-start(bf16[1,2,128,128]{3,2,1,0:T(8,128)(2,1)S(1)} %bitcast.76), channel_id=1, source_target_pairs={{8,0},{9,1},{10,2},{11,3},{12,4},{13,5},{14,6},{15,7},{16,8},{17,9... | collective-permute-start | bytes 196616 | tf_op jit(solution)/shard_map/ppermute | solution.py:25
  219.1 4.1 %collective-permute-start.16 = (bf16[256,1024]{0,1:T(8,128)(2,1)S(1)}, bf16[256,1024]{0,1:T(8,128)(2,1)S(1)}, u32[]{:S(2)}, u32[]{:S(2)}) collective-permute-start(bf16[256,1024]{0,1:T(8,128)(2,1)S(1)} %convert_element_type.44), channel_id=1, source_target_pairs={{0,1},{1,0},{2,3},{3,2},{4,5},{5,4},{6,7},{7,6},{8,9},{9,8},{10,11... | collective-permute-start | bytes 1572872 | tf_op jit(solution)/shard_map/ppermute | solution.py:31
  225.0 24.3 %collective-permute-start.17 = (bf16[512,1024]{0,1:T(8,128)(2,1)S(1)}, bf16[512,1024]{0,1:T(8,128)(2,1)S(1)}, u32[]{:S(2)}, u32[]{:S(2)}) collective-permute-start(bf16[512,1024]{0,1:T(8,128)(2,1)S(1)} %get-tuple-element.20), channel_id=1, source_target_pairs={{0,2},{1,3},{2,0},{3,1},{4,6},{5,7},{6,4},{7,5},{8,10},{9,11},{10,... | collective-permute-start | bytes 3145736 | tf_op jit(solution)/shard_map/ppermute | solution.py:31
  (10 other events, 115.3 us)
where the time goes:
time: 254 us; the launch traced here: 251 us
  waiting for transfers between devices  76.6 us (30%)
  starting transfers between devices  50.8 us (20%)
  other arithmetic  50.2 us (20%)
  local copies, waits for them, and re-layouts  39.1 us (15%)
  matrix products  32.9 us (13%)
    ppermute x16, waiting for transfers between devices, passed_along(): lax.ppermute(value, axis, [(source, source + steps) for source in range(l...  57 us
    ppermute x16, starting transfers between devices, passed_along(): lax.ppermute(value, axis, [(source, source + steps) for source in range(l...  47.9 us
    another operation x4, other arithmetic, local(): leaf_factor = jnp.linalg.cholesky(dense_diag[:, :redundant, :redundant])  23.6 us
    another operation x2, other arithmetic, lower_solve(): lax.linalg.triangular_solve(lower_factor, right_side, left_side=True, low...  20.4 us
    ppermute x2, waiting for transfers between devices, partner_2(): return lax.ppermute(value, axis, pairs)  19.6 us
    unnamed x51, local copies, waits for them, and re-layouts  19 us
    dot_general x1, matrix products, local(): jnp.einsum('lnac,lncb->lnab', half_proj, near_bases, preferred_element_ty...  12.5 us
    dot_general x1, matrix products, local(): jnp.einsum('lqbn,lnxy->lqxby', slot_hits.astype(jnp.float32), near_schur,...  7.79 us
  transfers between devices with their start and end apart: 18, of which 7 were waited for; matrix products, arithmetic and copies ran while one was open for 29% of the time, Pallas kernels for 0%

commit v1 on v0

v1 whole, which is shorter than its diff:
```python
import functools

import jax
import jax.numpy as jnp
from jax import lax
from jax.experimental import pallas as pl
from jax.experimental.pallas import tpu as pltpu
from jax.sharding import PartitionSpec as P

RANK = 128
REACH = 16
CHILDREN = 8
PANEL = 32
MESH = pl.DeviceIdType.MESH
highest = lax.Precision.HIGHEST


def matmul(a, b):
    return jnp.dot(a, b, preferred_element_type=jnp.float32)


def matmul_t(a, b, precision=None):
    return lax.dot_general(
        a, b, (((0,), (0,)), ((), ())), preferred_element_type=jnp.float32, precision=precision
    )


def factor_kernel(diag, bases, factor, panel, skeleton, shift, shift_t2, bases_t, work, rows):
    per_device, leaf_rows = bases.shape[0], bases.shape[1]
    red = leaf_rows - RANK
    wide = 2 * red + RANK
    row_id = lax.broadcasted_iota(jnp.int32, (red, red), 0)
    col_id = lax.broadcasted_iota(jnp.int32, (red, red), 1)
    low_corner = []
    for leaf in range(per_device):
        basis = bases[leaf]
        basis_t = basis.T
        bases_t[leaf] = basis_t
        half = matmul(basis_t, diag[leaf]).astype(jnp.bfloat16)
        dense = matmul(half, basis)
        top = dense[:red, :red]
        work[leaf, :, :red] = 0.5 * (top + top.T)
        work[leaf, :, red : red + RANK] = dense[:red, red:]
        work[leaf, :, red + RANK :] = (row_id == col_id).astype(jnp.float32)
        low_corner.append(dense[red:, red:])
    sub = lax.broadcasted_iota(jnp.int32, (PANEL, 1), 0)
    for start in range(0, red, PANEL):
        strips = [work[leaf, start : start + PANEL, :] for leaf in range(per_device)]
        for k in range(PANEL):
            for leaf in range(per_device):
                strip = strips[leaf]
                column = strip[:, start + k : start + k + 1]
                ratio = jnp.where(sub > k, column / column[k : k + 1], 0.0)
                strips[leaf] = strip - ratio * strip[k : k + 1, :]
        lane = lax.broadcasted_iota(jnp.int32, (PANEL, wide), 1)
        line = lax.broadcasted_iota(jnp.int32, (PANEL, wide), 0)
        for leaf in range(per_device):
            strip = strips[leaf]
            pivots = jnp.sum(jnp.where(lane == line + start, strip, 0.0), axis=1, keepdims=True)
            strip = strip * (1.0 / jnp.sqrt(pivots))
            rows[leaf, start : start + PANEL, :] = strip
            if start + PANEL < red:
                work[leaf] = work[leaf] - matmul_t(strip[:, :red], strip, highest)
    for leaf in range(per_device):
        upper = jnp.where(col_id >= row_id, rows[leaf, :, :red], 0.0)
        factor[leaf] = upper.T
        solved = rows[leaf, :, red : red + RANK]
        panel[leaf] = solved
        inverse = jnp.where(col_id <= row_id, rows[leaf, :, red + RANK :], 0.0)
        skeleton[leaf] = low_corner[leaf] - matmul_t(solved, solved, highest)
        moved = matmul_t(inverse, solved, highest)
        shift[leaf] = moved.astype(jnp.bfloat16)
        turned = moved.T.astype(jnp.bfloat16)
        shift_t2[leaf, :, :red] = turned
        shift_t2[leaf, :, red:] = turned


def window_kernel(
    chips, count, bases, shift, win_bases, win_shift, send, recv, pass_send, pass_recv, own_sem
):
    me = lax.axis_index("leaf")
    core = me % 2
    sibling = me + 1 - 2 * core
    offsets = [sign * step for step in range(chips, 0, -1) for sign in (1, -1)]
    pairs = ((bases, win_bases), (shift, win_shift))

    def inside(offset):
        other = me + 2 * offset
        return (other >= 0) & (other < count)

    barrier = pltpu.get_barrier_semaphore()
    pl.semaphore_signal(barrier, inc=1, device_id=(sibling,), device_id_type=MESH)
    for offset in offsets:

        @pl.when(inside(offset))
        def _(offset=offset):
            pl.semaphore_signal(barrier, inc=1, device_id=(me + 2 * offset,), device_id_type=MESH)

    peers = jnp.int32(1)
    for offset in offsets:
        peers = peers + inside(offset).astype(jnp.int32)
    pl.semaphore_wait(barrier, peers)

    def direct(kind, offset):
        source, window = pairs[kind]
        return pltpu.make_async_remote_copy(
            src_ref=source,
            dst_ref=window.at[2 * (chips - offset) + core],
            send_sem=send.at[kind, chips + offset],
            recv_sem=recv.at[kind, chips - offset],
            device_id=(me + 2 * offset,),
            device_id_type=MESH,
        )

    def arrival(kind, offset):
        source, window = pairs[kind]
        return pltpu.make_async_remote_copy(
            src_ref=source,
            dst_ref=window.at[2 * (chips + offset) + core],
            send_sem=send.at[kind, chips + offset],
            recv_sem=recv.at[kind, chips + offset],
            device_id=(sibling,),
            device_id_type=MESH,
        )

    def relay(kind, offset):
        source, window = pairs[kind]
        slot = 2 * (chips + offset) + core
        return pltpu.make_async_remote_copy(
            src_ref=source if offset == 0 else window.at[slot],
            dst_ref=window.at[slot],
            send_sem=pass_send.at[kind, chips + offset],
            recv_sem=pass_recv.at[kind, chips + offset],
            device_id=(sibling,),
            device_id_type=MESH,
        )

    def relayed(kind, offset):
        source, window = pairs[kind]
        slot = 2 * (chips + offset) + 1 - core
        return pltpu.make_async_remote_copy(
            src_ref=source,
            dst_ref=window.at[slot],
            send_sem=pass_send.at[kind, chips + offset],
            recv_sem=pass_recv.at[kind, chips + offset],
            device_id=(sibling,),
            device_id_type=MESH,
        )

    for kind in range(2):
        for offset in offsets:

            @pl.when(inside(offset))
            def _(kind=kind, offset=offset):
                direct(kind, offset).start()

        relay(kind, 0).start()
        source, window = pairs[kind]
        pltpu.make_async_copy(source, window.at[2 * chips + core], own_sem.at[kind]).start()

    for kind in range(2):
        for offset in offsets[::-1]:

            @pl.when(inside(offset))
            def _(kind=kind, offset=offset):
                arrival(kind, offset).wait_recv()
                relay(kind, offset).start()

    for kind in range(2):
        source, window = pairs[kind]
        pltpu.make_async_copy(source, window.at[2 * chips + core], own_sem.at[kind]).wait()
        relay(kind, 0).wait_send()
        relayed(kind, 0).wait_recv()
        for offset in offsets:

            @pl.when(inside(offset))
            def _(kind=kind, offset=offset):
                direct(kind, offset).wait_send()
                relay(kind, offset).wait_send()
                relayed(kind, offset).wait_recv()


def couple_kernel(
    chips,
    group,
    where,
    nbrs,
    parents,
    near,
    bases_t,
    shift_t2,
    skeleton,
    win_bases,
    win_shift,
    merged,
    diagonal,
):
    leaf, step = pl.program_id(0), pl.program_id(1)
    per_device = pl.num_programs(0)
    steps = pl.num_programs(1)
    red = bases_t.shape[1] - RANK
    me = where[0]
    number = me * per_device + leaf
    parent = number // CHILDREN
    targets = parents.shape[1]

    @pl.when(step == 0)
    def _():
        merged[...] = jnp.zeros_like(merged)
        place = pl.multiple_of((number % CHILDREN) * RANK, RANK)
        for q in range(targets):

            @pl.when(parents[parent, q] == parent)
            def _(q=q):
                merged[0, q, :, pl.ds(place, RANK)] = skeleton[0]

    @pl.when(nbrs[leaf, step * group] >= 0)
    def _():
        for k in range(group):
            other = nbrs[leaf, step * group + k]
            safe = jnp.where(other >= 0, other, number)
            owner = safe // per_device
            slot = (owner // 2 - me // 2 + chips) * 2 + owner % 2
            basis = win_bases[slot, safe % per_device]
            moved = win_shift[slot, safe % per_device]
            half = matmul(bases_t[0], near[0, k]).astype(jnp.bfloat16)
            right = matmul(half, basis[:, red:])
            left = matmul(half[red:], basis[:, :red])
            high = right[:red].astype(jnp.bfloat16)
            low = (right[:red] - high.astype(jnp.float32)).astype(jnp.bfloat16)
            first = matmul(shift_t2[0], jnp.concatenate([high, low], axis=0))
            high = left.astype(jnp.bfloat16)
            low = (left - high.astype(jnp.float32)).astype(jnp.bfloat16)
            second = matmul(
                jnp.concatenate([high, low], axis=1), jnp.concatenate([moved, moved], axis=0)
            )
            schur = right[red:] - first - second
            target = safe // CHILDREN
            q = jnp.int32(-1)
            for n in range(targets):
                q = jnp.where(parents[parent, n] == target, n, q)

            @pl.when((other >= 0) & (q >= 0))
            def _(schur=schur, q=q, safe=safe):
                place = pl.multiple_of((safe % CHILDREN) * RANK, RANK)
                merged[0, q, :, pl.ds(place, RANK)] = schur

    @pl.when(step == steps - 1)
    def _():
        diagonal[0] = merged[0, 0].astype(jnp.bfloat16)


def parent_kernel(size, own, diagonal, block, landed, send, recv):
    me = lax.axis_index("leaf")
    place = me % size
    base = me - place
    per_device, rank = own.shape[0], own.shape[2]
    width = per_device * rank
    barrier = pltpu.get_barrier_semaphore()
    for t in range(1, size):
        pl.semaphore_signal(
            barrier, inc=1, device_id=(base + (place + t) % size,), device_id_type=MESH
        )
    pl.semaphore_wait(barrier, size - 1)

    def copy(t):
        other = (place + t) % size
        return pltpu.make_async_remote_copy(
            src_ref=diagonal.at[:, :, pl.ds(pl.multiple_of(other * width, 128), width)],
            dst_ref=landed.at[size - t],
            send_sem=send.at[t],
            recv_sem=recv.at[size - t],
            device_id=(base + other,),
            device_id_type=MESH,
        )

    for t in range(1, size):
        copy(t).start()
    for t in range(size):
        other = (place + t) % size
        columns = pl.ds(pl.multiple_of(other * width, 128), width)
        mine = own[:, 0, :, columns].reshape(width, width)
        if t == 0:
            theirs = mine
        else:
            copy(size - t).wait_recv()
            theirs = landed[t].reshape(width, width).astype(jnp.float32)
        block[:, columns] = 0.5 * (mine + theirs.T)
    for t in range(1, size):
        copy(t).wait_send()


def local(count, near_blocks, diag_blocks, bases, leaf_nbrs, parent_nbrs):
    per_device, leaf_rows = bases.shape[0], bases.shape[1]
    red = leaf_rows - RANK
    slots = near_blocks.shape[1]
    targets = parent_nbrs.shape[1]
    span = REACH // per_device
    chips = (span + 1) // 2
    vmem = pl.BlockSpec(memory_space=pltpu.VMEM)
    anywhere = pl.BlockSpec(memory_space=pl.ANY)
    f32, bf16 = jnp.float32, jnp.bfloat16

    def out(shape, dtype):
        return jax.ShapeDtypeStruct(shape, dtype)

    factor, panel, skeleton, shift, shift_t2, bases_t = pl.pallas_call(
        factor_kernel,
        out_shape=(
            out((per_device, red, red), f32),
            out((per_device, red, RANK), f32),
            out((per_device, RANK, RANK), f32),
            out((per_device, red, RANK), bf16),
            out((per_device, RANK, 2 * red), bf16),
            out(bases.shape, bf16),
        ),
        in_specs=[vmem] * 2,
        out_specs=(vmem,) * 6,
        scratch_shapes=[
            pltpu.VMEM((per_device, red, 2 * red + RANK), f32),
            pltpu.VMEM((per_device, red, 2 * red + RANK), f32),
        ],
        name="factor",
    )(diag_blocks, bases)

    window = 2 * (2 * chips + 1)
    sems = pltpu.SemaphoreType.DMA((2, 2 * chips + 1))
    win_bases, win_shift = pl.pallas_call(
        functools.partial(window_kernel, chips, count),
        out_shape=(
            out((window,) + bases.shape, bf16),
            out((window,) + shift.shape, bf16),
        ),
        in_specs=[vmem] * 2,
        out_specs=(anywhere,) * 2,
        scratch_shapes=[sems, sems, sems, sems, pltpu.SemaphoreType.DMA((2,))],
        compiler_params=pltpu.CompilerParams(collective_id=0, has_side_effects=True),
        name="window",
    )(bases, shift)

    group = 2 if slots % 2 == 0 else 1
    where = lax.axis_index("leaf").astype(jnp.int32).reshape(1)

    def near_map(leaf, step, where, nbrs, parents):
        return leaf, jnp.where(nbrs[leaf, step * group] >= 0, step, 0), 0, 0

    def by_leaf(rank):
        return lambda leaf, step, *_: (leaf,) + (0,) * (rank - 1)

    merged, diagonal = pl.pallas_call(
        functools.partial(couple_kernel, chips, group),
        out_shape=(
            out((per_device, targets, RANK, CHILDREN * RANK), f32),
            out((per_device, RANK, CHILDREN * RANK), bf16),
        ),
        grid_spec=pltpu.PrefetchScalarGridSpec(
            num_scalar_prefetch=3,
            grid=(per_device, slots // group),
            in_specs=[
                pl.BlockSpec((1, group, leaf_rows, leaf_rows), near_map),
                pl.BlockSpec((1, leaf_rows, leaf_rows), by_leaf(3)),
                pl.BlockSpec((1, RANK, 2 * red), by_leaf(3)),
                pl.BlockSpec((1, RANK, RANK), by_leaf(3)),
                vmem,
                vmem,
            ],
            out_specs=(
                pl.BlockSpec((1, targets, RANK, CHILDREN * RANK), by_leaf(4)),
                pl.BlockSpec((1, RANK, CHILDREN * RANK), by_leaf(3)),
            ),
        ),
        compiler_params=pltpu.CompilerParams(
            dimension_semantics=("arbitrary", "arbitrary"), vmem_limit_bytes=48 << 20
        ),
        name="couple",
    )(where, leaf_nbrs, parent_nbrs, near_blocks, bases_t, shift_t2, skeleton, win_bases, win_shift)

    size = CHILDREN // per_device
    width = per_device * RANK
    parent_block = pl.pallas_call(
        functools.partial(parent_kernel, size),
        out_shape=out((width, CHILDREN * RANK), f32),
        grid=(1,),
        in_specs=[
            pl.BlockSpec((per_device, 1, RANK, CHILDREN * RANK), lambda i: (0, 0, 0, 0)),
            vmem,
        ],
        out_specs=vmem,
        scratch_shapes=[
            pltpu.VMEM((size, per_device, RANK, width), bf16),
            pltpu.SemaphoreType.DMA((size,)),
            pltpu.SemaphoreType.DMA((size,)),
        ],
        compiler_params=pltpu.CompilerParams(collective_id=1, has_side_effects=True),
        name="parent",
    )(merged, diagonal)
    return factor, panel, merged, parent_block


def solution(mesh):
    count = mesh.shape["leaf"]
    in_specs = (
        P("leaf", None, None, None),
        P("leaf", None, None),
        P("leaf", None, None),
        P("leaf", None),
        P(),
    )
    out_specs = (
        P("leaf", None, None),
        P("leaf", None, None),
        P("leaf", None, None, None),
        P("leaf", None),
    )
    return jax.shard_map(
        functools.partial(local, count),
        mesh=mesh,
        in_specs=in_specs,
        out_specs=out_specs,
        check_vma=False,
    )
```

time: 254 us -> 107 us (0.42)
  Pallas kernels: 0 us -> 97.2 us
  waiting for transfers between devices: 76.6 us -> 0 us
  starting transfers between devices: 50.8 us -> 0 us
  other arithmetic: 50.2 us -> 0 us
  matrix products: 32.9 us -> 0 us
  local copies, waits for them, and re-layouts: 39.1 us -> 8.48 us
    pallas_call x0 -> x4, Pallas kernels: none -> 97.2 us  [the longest x1 40.4 us: local(): pl.pallas_call(functools.partial(window_kernel, chips, count), out_shape=...]
    ppermute x18 -> x0, waiting for transfers between devices: 76.6 us -> none  [the longest x16 57 us: passed_along(): lax.ppermute(value, axis, [(source, source + steps) for source in range(l...]
    ppermute x18 -> x0, starting transfers between devices: 50.8 us -> none  [the longest x16 47.9 us: passed_along(): lax.ppermute(value, axis, [(source, source + steps) for source in range(l...]
    another operation x6 -> x0, other arithmetic: 44 us -> none  [the longest x4 23.6 us: local(): leaf_factor = jnp.linalg.cholesky(dense_diag[:, :redundant, :redundant])]
    dot_general x6 -> x0, matrix products: 32.3 us -> none  [the longest x1 12.5 us: local(): jnp.einsum('lnac,lncb->lnab', half_proj, near_bases, preferred_element_ty...]
    unnamed x51 -> x15, local copies, waits for them, and re-layouts: 19 us -> 8.48 us
    gather x2 -> x0, local copies, waits for them, and re-layouts: 8.14 us -> none  [the longest x1 7.27 us: local(): near_bases = win_bases[window_slot]]
    add x1 -> x0, local copies, waits for them, and re-layouts: 6.3 us -> none  [local(): parent_rows + self_hit.astype(jnp.float32)[:, :, None, :, None] * skeleto...]
  transfers between devices with their start and end apart: 18 -> 0, of which waited for: 7 -> 0; matrix products, arithmetic and copies ran while one was open for 29% -> 0% of each run, Pallas kernels for 0% -> 0%
where the time goes in v1:
time: 107 us; the launch traced here: 106 us
  Pallas kernels  97.2 us (91%)
  local copies, waits for them, and re-layouts  8.48 us (8%)
    pallas_call x1, Pallas kernels, local(): pl.pallas_call(functools.partial(window_kernel, chips, count), out_shape=...  40.4 us
    pallas_call x1, Pallas kernels, local(): pl.pallas_call(functools.partial(couple_kernel, chips, group), out_shape=...  21.6 us
    pallas_call x1, Pallas kernels, local(): pl.pallas_call(functools.partial(parent_kernel, size), out_shape=out((wid...  20.5 us
    pallas_call x1, Pallas kernels, local(): pl.pallas_call(factor_kernel, out_shape=(out((per_device, red, red), f32)...  14.7 us
    unnamed x15, local copies, waits for them, and re-layouts  8.48 us

profile of v1, /device:TPU:23, one launch (start us, length us, event | category | flops | bytes accessed | tf_op | source)
XLA Modules:
  0.0 106.4 jit_solution(9830321446350982456)
XLA Ops:
  0.6 14.7 %factor.1 = (f32[2,128,128]{2,1,0:T(8,128)}, f32[2,128,128]{2,1,0:T(8,128)}, f32[2,128,128]{2,1,0:T(8,128)}, bf16[2,128,128]{2,1,0:T(8,128)(2,1)}, bf16[2,128,25...) custom-call(bf16[2,256,256]{2,1,0:T(8,128)(2,1)} %diag.1, bf16[2,256,256]{2,1,0:T(8,128)(2,1)} %bases.3), custom_call_target="tpu_custom_call" | custom-call | tf_op jit(solution)/shard_map/factor/pallas_call | solution.py:307
  15.3 40.4 %window.1 = (bf16[18,2,256,256]{3,2,1,0:T(8,128)(2,1)}, bf16[18,2,128,128]{3,2,1,0:T(8,128)(2,1)}) custom-call(bf16[2,256,256]{2,1,0:T(8,128)(2,1)} %bases.3, bf16[2,128,128]{2,1,0:T(8,128)(2,1)} %get-tuple-element.19.shift), custom_call_target="tpu_custom_call" | custom-call | tf_op jit(solution)/shard_map/window/pallas_call | solution.py:328
  55.7 0.0 copy-start
  55.7 1.3 %copy-done = bf16[18,2,128,128]{3,2,1,0:T(8,128)(2,1)S(1)} copy-done((bf16[18,2,128,128]{3,2,1,0:T(8,128)(2,1)S(1)}, bf16[18,2,128,128]{3,2,1,0:T(8,128)(2,1)}, u32[]{:S(2)}) %copy-start) | copy-done | bytes 1179672
  57.0 0.0 copy-start.2
  57.0 0.9 copy-done.2
  58.0 0.0 copy-start.3
  58.0 0.9 copy-done.3
  58.9 0.0 copy-start.4
  58.9 0.9 copy-done.4
  59.8 0.0 copy-start.5
  59.8 0.7 copy-done.5
  60.5 0.0 copy-start.6
  60.5 0.7 copy-done.6
  61.1 21.6 %couple.1 = (f32[2,5,128,1024]{3,2,1,0:T(8,128)}, bf16[2,128,1024]{2,1,0:T(8,128)(2,1)S(1)}) custom-call(s32[1]{0:T(128)} %bitcast.where, s32[2,26]{1,0:T(2,128)S(1)} %copy-done.6, s32[8,5]{1,0:T(8,128)S(1)} %copy-done.5, bf16[2,26,256,256]{3,2,1,0:T(8,128)(2,1)} %near.1, bf16[2,256,256]{2,1,0:T(8,128)(2,1)S(1)} %copy-done.2, ...), custom_call_target="tpu_custom_call" | custom-call | tf_op jit(solution)/shard_map/couple/pallas_call | solution.py:350
  82.7 0.0 copy-start.1
  82.7 0.8 copy-done.1
  83.5 20.5 %parent.1 = f32[256,1024]{1,0:T(8,128)} custom-call(f32[2,5,128,1024]{3,2,1,0:T(8,128)} %get-tuple-element.30.own, bf16[2,128,1024]{2,1,0:T(8,128)(2,1)} %copy-done.1), custom_call_target="tpu_custom_call" | custom-call | tf_op jit(solution)/shard_map/parent/pallas_call | solution.py:380
  104.1 2.3 %copy.10 = f32[256,1024]{1,0:T(8,128)} copy(f32[256,1024]{1,0:T(8,128)} %parent.1) | data formatting | bytes 2097152
Async XLA Ops:
  55.7 1.3 %copy-start = (bf16[18,2,128,128]{3,2,1,0:T(8,128)(2,1)S(1)}, bf16[18,2,128,128]{3,2,1,0:T(8,128)(2,1)}, u32[]{:S(2)}) copy-start(bf16[18,2,128,128]{3,2,1,0:T(8,128)(2,1)} %get-tuple-element.21.win_shift) | copy-start | bytes 3538948
  57.0 0.9 copy-start.2
  58.0 0.9 copy-start.3
  58.9 0.9 copy-start.4
  59.8 0.7 copy-start.5
  60.5 0.7 copy-start.6
  82.7 0.8 copy-start.1

commit v2 on v1

--- a/solution.py
+++ b/solution.py
@@ -25,7 +25,7 @@
     )
 
 
-def factor_kernel(diag, bases, factor, panel, skeleton, shift, shift_t2, bases_t, work, rows):
+def eliminate(diag, bases, factor, panel, skeleton, shift, shift_t2, bases_t, work, rows):
     per_device, leaf_rows = bases.shape[0], bases.shape[1]
     red = leaf_rows - RANK
     wide = 2 * red + RANK
@@ -62,22 +62,59 @@
             if start + PANEL < red:
                 work[leaf] = work[leaf] - matmul_t(strip[:, :red], strip, highest)
     for leaf in range(per_device):
-        upper = jnp.where(col_id >= row_id, rows[leaf, :, :red], 0.0)
-        factor[leaf] = upper.T
         solved = rows[leaf, :, red : red + RANK]
-        panel[leaf] = solved
         inverse = jnp.where(col_id <= row_id, rows[leaf, :, red + RANK :], 0.0)
-        skeleton[leaf] = low_corner[leaf] - matmul_t(solved, solved, highest)
         moved = matmul_t(inverse, solved, highest)
         shift[leaf] = moved.astype(jnp.bfloat16)
         turned = moved.T.astype(jnp.bfloat16)
         shift_t2[leaf, :, :red] = turned
         shift_t2[leaf, :, red:] = turned
+    for leaf in range(per_device):
+        solved = rows[leaf, :, red : red + RANK]
+        panel[leaf] = solved
+        skeleton[leaf] = low_corner[leaf] - matmul_t(solved, solved, highest)
+        upper = jnp.where(col_id >= row_id, rows[leaf, :, :red], 0.0)
+        factor[leaf] = upper.T
 
 
 def window_kernel(
-    chips, count, bases, shift, win_bases, win_shift, send, recv, pass_send, pass_recv, own_sem
+    chips,
+    count,
+    diag,
+    bases,
+    near,
+    factor,
+    panel,
+    skeleton,
+    shift_t2,
+    halves,
+    win_bases,
+    win_shift,
+    shift,
+    bases_t,
+    work,
+    rows,
+    near_in,
+    half_out,
+    send,
+    recv,
+    pass_send,
+    pass_recv,
+    own_sem,
+    near_sem,
+    half_sem,
 ):
+    per_device, slots = near_in.shape[0], near_in.shape[1]
+    fetches = [
+        pltpu.make_async_copy(near.at[leaf], near_in.at[leaf], near_sem.at[leaf])
+        for leaf in range(per_device)
+    ]
+    stores = [
+        pltpu.make_async_copy(
+            half_out.at[leaf], halves.at[leaf, pl.ds(0, slots)], half_sem.at[leaf]
+        )
+        for leaf in range(per_device)
+    ]
     me = lax.axis_index("leaf")
     core = me % 2
     sibling = me + 1 - 2 * core
@@ -147,24 +184,47 @@
             device_id_type=MESH,
         )
 
-    for kind in range(2):
+    def dispatch(kind):
         for offset in offsets:
 
             @pl.when(inside(offset))
-            def _(kind=kind, offset=offset):
+            def _(offset=offset):
                 direct(kind, offset).start()
 
         relay(kind, 0).start()
         source, window = pairs[kind]
         pltpu.make_async_copy(source, window.at[2 * chips + core], own_sem.at[kind]).start()
 
-    for kind in range(2):
-        for offset in offsets[::-1]:
-
-            @pl.when(inside(offset))
-            def _(kind=kind, offset=offset):
-                arrival(kind, offset).wait_recv()
-                relay(kind, offset).start()
+    def hand_on(kind, offset):
+        @pl.when(inside(offset))
+        def _():
+            arrival(kind, offset).wait_recv()
+            relay(kind, offset).start()
+
+    def project(first, last):
+        @pl.loop(first, last)
+        def _(n):
+            for leaf in range(per_device):
+                half_out[leaf, n] = matmul(bases_t[leaf], near_in[leaf, n]).astype(jnp.bfloat16)
+
+    dispatch(0)
+    for fetch in fetches:
+        fetch.start()
+    eliminate(diag, bases, factor, panel, skeleton, shift, shift_t2, bases_t, work, rows)
+    dispatch(1)
+    for fetch in fetches:
+        fetch.wait()
+    nearest = offsets[::-1]
+    done = 0
+    for turn, offset in enumerate(nearest):
+        hand_on(0, offset)
+        upto = slots * (turn + 1) // len(nearest)
+        project(done, upto)
+        done = upto
+    for store in stores:
+        store.start()
+    for offset in nearest:
+        hand_on(1, offset)
 
     for kind in range(2):
         source, window = pairs[kind]
@@ -179,15 +239,18 @@
                 relay(kind, offset).wait_send()
                 relayed(kind, offset).wait_recv()
 
+    for store in stores:
+        store.wait()
+
 
 def couple_kernel(
     chips,
     group,
+    slots,
     where,
     nbrs,
     parents,
-    near,
-    bases_t,
+    halves,
     shift_t2,
     skeleton,
     win_bases,
@@ -198,7 +261,7 @@
     leaf, step = pl.program_id(0), pl.program_id(1)
     per_device = pl.num_programs(0)
     steps = pl.num_programs(1)
-    red = bases_t.shape[1] - RANK
+    red = shift_t2.shape[2] // 2
     me = where[0]
     number = me * per_device + leaf
     parent = number // CHILDREN
@@ -216,14 +279,16 @@
 
     @pl.when(nbrs[leaf, step * group] >= 0)
     def _():
+        results = []
         for k in range(group):
-            other = nbrs[leaf, step * group + k]
+            n = step * group + k
+            other = jnp.where(n < slots, nbrs[leaf, jnp.minimum(n, slots - 1)], -1)
             safe = jnp.where(other >= 0, other, number)
             owner = safe // per_device
             slot = (owner // 2 - me // 2 + chips) * 2 + owner % 2
             basis = win_bases[slot, safe % per_device]
             moved = win_shift[slot, safe % per_device]
-            half = matmul(bases_t[0], near[0, k]).astype(jnp.bfloat16)
+            half = halves[0, k]
             right = matmul(half, basis[:, red:])
             left = matmul(half[red:], basis[:, :red])
             high = right[:red].astype(jnp.bfloat16)
@@ -234,15 +299,15 @@
             second = matmul(
                 jnp.concatenate([high, low], axis=1), jnp.concatenate([moved, moved], axis=0)
             )
-            schur = right[red:] - first - second
-            target = safe // CHILDREN
             q = jnp.int32(-1)
-            for n in range(targets):
-                q = jnp.where(parents[parent, n] == target, n, q)
+            for place in range(targets):
+                q = jnp.where(parents[parent, place] == safe // CHILDREN, place, q)
+            results.append((right[red:] - first - second, other, q))
+        for schur, other, q in results:
 
             @pl.when((other >= 0) & (q >= 0))
-            def _(schur=schur, q=q, safe=safe):
-                place = pl.multiple_of((safe % CHILDREN) * RANK, RANK)
+            def _(schur=schur, other=other, q=q):
+                place = pl.multiple_of((other % CHILDREN) * RANK, RANK)
                 merged[0, q, :, pl.ds(place, RANK)] = schur
 
     @pl.when(step == steps - 1)
@@ -304,61 +369,64 @@
     def out(shape, dtype):
         return jax.ShapeDtypeStruct(shape, dtype)
 
-    factor, panel, skeleton, shift, shift_t2, bases_t = pl.pallas_call(
-        factor_kernel,
+    group = 4
+    steps = -(-slots // group)
+    window = 2 * (2 * chips + 1)
+    sems = pltpu.SemaphoreType.DMA((2, 2 * chips + 1))
+    leaf_sems = pltpu.SemaphoreType.DMA((per_device,))
+    factor, panel, skeleton, shift_t2, halves, win_bases, win_shift = pl.pallas_call(
+        functools.partial(window_kernel, chips, count),
         out_shape=(
             out((per_device, red, red), f32),
             out((per_device, red, RANK), f32),
             out((per_device, RANK, RANK), f32),
-            out((per_device, red, RANK), bf16),
             out((per_device, RANK, 2 * red), bf16),
-            out(bases.shape, bf16),
+            out((per_device, steps * group) + near_blocks.shape[2:], bf16),
+            out((window,) + bases.shape, bf16),
+            out((window, per_device, red, RANK), bf16),
         ),
-        in_specs=[vmem] * 2,
-        out_specs=(vmem,) * 6,
+        in_specs=[vmem, vmem, anywhere],
+        out_specs=(vmem,) * 4 + (anywhere,) * 3,
         scratch_shapes=[
+            pltpu.VMEM((per_device, red, RANK), bf16),
+            pltpu.VMEM(bases.shape, bf16),
             pltpu.VMEM((per_device, red, 2 * red + RANK), f32),
             pltpu.VMEM((per_device, red, 2 * red + RANK), f32),
+            pltpu.VMEM(near_blocks.shape, bf16),
+            pltpu.VMEM(near_blocks.shape, bf16),
+            sems,
+            sems,
+            sems,
+            sems,
+            pltpu.SemaphoreType.DMA((2,)),
+            leaf_sems,
+            leaf_sems,
         ],
-        name="factor",
-    )(diag_blocks, bases)
-
-    window = 2 * (2 * chips + 1)
-    sems = pltpu.SemaphoreType.DMA((2, 2 * chips + 1))
-    win_bases, win_shift = pl.pallas_call(
-        functools.partial(window_kernel, chips, count),
-        out_shape=(
-            out((window,) + bases.shape, bf16),
-            out((window,) + shift.shape, bf16),
+        compiler_params=pltpu.CompilerParams(
+            collective_id=0, has_side_effects=True, vmem_limit_bytes=66_000_000
         ),
-        in_specs=[vmem] * 2,
-        out_specs=(anywhere,) * 2,
-        scratch_shapes=[sems, sems, sems, sems, pltpu.SemaphoreType.DMA((2,))],
-        compiler_params=pltpu.CompilerParams(collective_id=0, has_side_effects=True),
         name="window",
-    )(bases, shift)
-
-    group = 2 if slots % 2 == 0 else 1
+    )(diag_blocks, bases, near_blocks)
+
     where = lax.axis_index("leaf").astype(jnp.int32).reshape(1)
 
-    def near_map(leaf, step, where, nbrs, parents):
+    def half_map(leaf, step, where, nbrs, parents):
         return leaf, jnp.where(nbrs[leaf, step * group] >= 0, step, 0), 0, 0
 
     def by_leaf(rank):
         return lambda leaf, step, *_: (leaf,) + (0,) * (rank - 1)
 
     merged, diagonal = pl.pallas_call(
-        functools.partial(couple_kernel, chips, group),
+        functools.partial(couple_kernel, chips, group, slots),
         out_shape=(
             out((per_device, targets, RANK, CHILDREN * RANK), f32),
             out((per_device, RANK, CHILDREN * RANK), bf16),
         ),
         grid_spec=pltpu.PrefetchScalarGridSpec(
             num_scalar_prefetch=3,
-            grid=(per_device, slots // group),
+            grid=(per_device, steps),
             in_specs=[
-                pl.BlockSpec((1, group, leaf_rows, leaf_rows), near_map),
-                pl.BlockSpec((1, leaf_rows, leaf_rows), by_leaf(3)),
+                pl.BlockSpec((1, group, leaf_rows, leaf_rows), half_map),
                 pl.BlockSpec((1, RANK, 2 * red), by_leaf(3)),
                 pl.BlockSpec((1, RANK, RANK), by_leaf(3)),
                 vmem,
@@ -370,10 +438,10 @@
             ),
         ),
         compiler_params=pltpu.CompilerParams(
-            dimension_semantics=("arbitrary", "arbitrary"), vmem_limit_bytes=48 << 20
+            dimension_semantics=("arbitrary", "arbitrary"), vmem_limit_bytes=66_000_000
         ),
         name="couple",
-    )(where, leaf_nbrs, parent_nbrs, near_blocks, bases_t, shift_t2, skeleton, win_bases, win_shift)
+    )(where, leaf_nbrs, parent_nbrs, halves, shift_t2, skeleton, win_bases, win_shift)
 
     size = CHILDREN // per_device
     width = per_device * RANK

time: 107 us -> 79.5 us (0.74)
  Pallas kernels: 97.2 us -> 74.1 us
  local copies, waits for them, and re-layouts: 8.48 us -> 3.63 us
    pallas_call x2 -> x1, Pallas kernels: 36.3 us -> 19 us  [local(): pl.pallas_call(functools.partial(couple_kernel, chips, group, slots), out...]
    pallas_call x1, Pallas kernels: 20.5 us -> 12.7 us  [local(): pl.pallas_call(functools.partial(parent_kernel, size), out_shape=out((wid...]
    unnamed x15 -> x7, local copies, waits for them, and re-layouts: 8.48 us -> 3.63 us
    pallas_call x1, Pallas kernels: 40.4 us -> 42.4 us  [local(): pl.pallas_call(functools.partial(window_kernel, chips, count), out_shape=...]
where the time goes in v2:
time: 79.5 us; the launch traced here: 78.4 us
  Pallas kernels  74.1 us (93%)
  local copies, waits for them, and re-layouts  3.63 us (5%)
    pallas_call x1, Pallas kernels, local(): pl.pallas_call(functools.partial(window_kernel, chips, count), out_shape=...  42.4 us
    pallas_call x1, Pallas kernels, local(): pl.pallas_call(functools.partial(couple_kernel, chips, group, slots), out...  19 us
    pallas_call x1, Pallas kernels, local(): pl.pallas_call(functools.partial(parent_kernel, size), out_shape=out((wid...  12.7 us
    unnamed x7, local copies, waits for them, and re-layouts  3.63 us

profile of v2, /device:TPU:23, one launch (start us, length us, event | category | flops | bytes accessed | tf_op | source)
XLA Modules:
  0.0 78.4 jit_solution(2460821973233992953)
XLA Ops:
  0.6 42.4 %window.1 = (f32[2,128,128]{2,1,0:T(8,128)}, f32[2,128,128]{2,1,0:T(8,128)}, f32[2,128,128]{2,1,0:T(8,128)}, bf16[2,128,256]{2,1,0:T(8,128)(2,1)}, bf16[2,28,256...) custom-call(bf16[2,256,256]{2,1,0:T(8,128)(2,1)} %diag.1, ...), custom_call_target="tpu_custom_call" | custom-call | tf_op jit(solution)/shard_map/window/pallas_call | solution.py:377
  43.0 19.0 %couple.1 = (f32[2,5,128,1024]{3,2,1,0:T(8,128)}, bf16[2,128,1024]{2,1,0:T(8,128)(2,1)}) custom-call(s32[1]{0:T(128)} %bitcast.where, s32[2,26]{1,0:T(2,128)} %nbrs.1, s32[8,5]{1,0:T(8,128)} %parents.1, bf16[2,28,256,256]{3,2,1,0:T(8,128)(2,1)} %get-tuple-element.15.halves, bf16[2,128,256]{2,1,0:T(8,128)(2,1)} %get-tuple-element.16.shift_t2, ...), custom_call_target="tpu_custom_call" | custom-call | tf_op jit(solution)/shard_map/couple/pallas_call | solution.py:419
  62.0 0.0 copy-start.1
  62.0 0.0 copy-start
  62.1 12.7 %parent.1 = f32[256,1024]{1,0:T(8,128)} custom-call(f32[2,5,128,1024]{3,2,1,0:T(8,128)} %get-tuple-element.28.own, bf16[2,128,1024]{2,1,0:T(8,128)(2,1)} %get-tuple-element.21.diagonal), custom_call_target="tpu_custom_call" | custom-call | tf_op jit(solution)/shard_map/parent/pallas_call | solution.py:448
  74.8 0.0 copy-done.1
  74.8 0.7 copy.12
  75.4 0.0 copy-done
  75.4 0.7 copy.13
  76.1 2.3 %copy.14 = f32[256,1024]{1,0:T(8,128)} copy(f32[256,1024]{1,0:T(8,128)} %parent.1) | data formatting | bytes 2097152
Async XLA Ops:
  62.0 12.7 %copy-start.1 = (f32[2,128,128]{2,1,0:T(8,128)S(1)}, f32[2,128,128]{2,1,0:T(8,128)}, u32[]{:S(2)}) copy-start(f32[2,128,128]{2,1,0:T(8,128)} %get-tuple-element.26) | copy-start | bytes 393220
  62.0 13.4 %copy-start = (f32[2,128,128]{2,1,0:T(8,128)S(1)}, f32[2,128,128]{2,1,0:T(8,128)}, u32[]{:S(2)}) copy-start(f32[2,128,128]{2,1,0:T(8,128)} %get-tuple-element.27) | copy-start | bytes 393220

commit v3 on v2

--- a/solution.py
+++ b/solution.py
@@ -214,16 +214,15 @@
     dispatch(1)
     for fetch in fetches:
         fetch.wait()
-    nearest = offsets[::-1]
     done = 0
-    for turn, offset in enumerate(nearest):
+    for turn, offset in enumerate(offsets):
         hand_on(0, offset)
-        upto = slots * (turn + 1) // len(nearest)
+        upto = slots * (turn + 1) // len(offsets)
         project(done, upto)
         done = upto
     for store in stores:
         store.start()
-    for offset in nearest:
+    for offset in offsets:
         hand_on(1, offset)
 
     for kind in range(2):
@@ -243,21 +242,13 @@
         store.wait()
 
 
-def couple_kernel(
-    chips,
-    group,
-    slots,
-    where,
-    nbrs,
-    parents,
-    halves,
-    shift_t2,
-    skeleton,
-    win_bases,
-    win_shift,
-    merged,
-    diagonal,
-):
+def neighbour(slots, nbrs, leaf, n):
+    return jnp.where(n < slots, nbrs[leaf, jnp.minimum(n, slots - 1)], -1)
+
+
+def couple_kernel(group, slots, where, nbrs, parents, halves, shift_t2, skeleton, *rest):
+    win_bases, win_shift = rest[:group], rest[group : 2 * group]
+    factor, panel, merged, diagonal, factor_out, panel_out = rest[2 * group :]
     leaf, step = pl.program_id(0), pl.program_id(1)
     per_device = pl.num_programs(0)
     steps = pl.num_programs(1)
@@ -270,6 +261,8 @@
     @pl.when(step == 0)
     def _():
         merged[...] = jnp.zeros_like(merged)
+        factor_out[...] = factor[...]
+        panel_out[...] = panel[...]
         place = pl.multiple_of((number % CHILDREN) * RANK, RANK)
         for q in range(targets):
 
@@ -281,13 +274,9 @@
     def _():
         results = []
         for k in range(group):
-            n = step * group + k
-            other = jnp.where(n < slots, nbrs[leaf, jnp.minimum(n, slots - 1)], -1)
-            safe = jnp.where(other >= 0, other, number)
-            owner = safe // per_device
-            slot = (owner // 2 - me // 2 + chips) * 2 + owner % 2
-            basis = win_bases[slot, safe % per_device]
-            moved = win_shift[slot, safe % per_device]
+            other = neighbour(slots, nbrs, leaf, step * group + k)
+            basis = win_bases[k][0, 0]
+            moved = win_shift[k][0, 0]
             half = halves[0, k]
             right = matmul(half, basis[:, red:])
             left = matmul(half[red:], basis[:, :red])
@@ -301,7 +290,7 @@
             )
             q = jnp.int32(-1)
             for place in range(targets):
-                q = jnp.where(parents[parent, place] == safe // CHILDREN, place, q)
+                q = jnp.where(parents[parent, place] == other // CHILDREN, place, q)
             results.append((right[red:] - first - second, other, q))
         for schur, other, q in results:
 
@@ -315,12 +304,11 @@
         diagonal[0] = merged[0, 0].astype(jnp.bfloat16)
 
 
-def parent_kernel(size, own, diagonal, block, landed, send, recv):
+def parent_kernel(size, diagonal, landed, send, recv):
     me = lax.axis_index("leaf")
     place = me % size
     base = me - place
-    per_device, rank = own.shape[0], own.shape[2]
-    width = per_device * rank
+    width = landed.shape[3]
     barrier = pltpu.get_barrier_semaphore()
     for t in range(1, size):
         pl.semaphore_signal(
@@ -328,11 +316,11 @@
         )
     pl.semaphore_wait(barrier, size - 1)
 
-    def copy(t):
+    def copy(t, source):
         other = (place + t) % size
         return pltpu.make_async_remote_copy(
             src_ref=diagonal.at[:, :, pl.ds(pl.multiple_of(other * width, 128), width)],
-            dst_ref=landed.at[size - t],
+            dst_ref=landed.at[source],
             send_sem=send.at[t],
             recv_sem=recv.at[size - t],
             device_id=(base + other,),
@@ -340,19 +328,24 @@
         )
 
     for t in range(1, size):
-        copy(t).start()
-    for t in range(size):
-        other = (place + t) % size
-        columns = pl.ds(pl.multiple_of(other * width, 128), width)
-        mine = own[:, 0, :, columns].reshape(width, width)
-        if t == 0:
-            theirs = mine
-        else:
-            copy(size - t).wait_recv()
-            theirs = landed[t].reshape(width, width).astype(jnp.float32)
-        block[:, columns] = 0.5 * (mine + theirs.T)
+        copy(t, place).start()
     for t in range(1, size):
-        copy(t).wait_send()
+        copy(t, (place + size - t) % size).wait_recv()
+    for t in range(1, size):
+        copy(t, place).wait_send()
+
+
+def symmetric_kernel(size, where, own, landed, block):
+    width = block.shape[0]
+    mine = own[:, 0].reshape(width, width)
+
+    @pl.when(pl.program_id(0) == where[0] % size)
+    def _():
+        block[...] = 0.5 * (mine + mine.T)
+
+    @pl.when(pl.program_id(0) != where[0] % size)
+    def _():
+        block[...] = 0.5 * (mine + landed[0].reshape(width, width).astype(jnp.float32).T)
 
 
 def local(count, near_blocks, diag_blocks, bases, leaf_nbrs, parent_nbrs):
@@ -413,14 +406,27 @@
     def half_map(leaf, step, where, nbrs, parents):
         return leaf, jnp.where(nbrs[leaf, step * group] >= 0, step, 0), 0, 0
 
+    def window_map(k):
+        def index(leaf, step, where, nbrs, parents):
+            me = where[0]
+            other = neighbour(slots, nbrs, leaf, step * group + k)
+            other = jnp.where(other >= 0, other, me * per_device + leaf)
+            owner = other // per_device
+            slot = (owner // 2 - me // 2 + chips) * 2 + owner % 2
+            return slot, other % per_device, 0, 0
+
+        return index
+
     def by_leaf(rank):
         return lambda leaf, step, *_: (leaf,) + (0,) * (rank - 1)
 
-    merged, diagonal = pl.pallas_call(
-        functools.partial(couple_kernel, chips, group, slots),
+    merged, diagonal, factor, panel = pl.pallas_call(
+        functools.partial(couple_kernel, group, slots),
         out_shape=(
             out((per_device, targets, RANK, CHILDREN * RANK), f32),
             out((per_device, RANK, CHILDREN * RANK), bf16),
+            out(factor.shape, f32),
+            out(panel.shape, f32),
         ),
         grid_spec=pltpu.PrefetchScalarGridSpec(
             num_scalar_prefetch=3,
@@ -429,39 +435,69 @@
                 pl.BlockSpec((1, group, leaf_rows, leaf_rows), half_map),
                 pl.BlockSpec((1, RANK, 2 * red), by_leaf(3)),
                 pl.BlockSpec((1, RANK, RANK), by_leaf(3)),
-                vmem,
-                vmem,
+            ]
+            + [pl.BlockSpec((1, 1, leaf_rows, leaf_rows), window_map(k)) for k in range(group)]
+            + [pl.BlockSpec((1, 1, red, RANK), window_map(k)) for k in range(group)]
+            + [
+                pl.BlockSpec((1, red, red), by_leaf(3)),
+                pl.BlockSpec((1, red, RANK), by_leaf(3)),
             ],
             out_specs=(
                 pl.BlockSpec((1, targets, RANK, CHILDREN * RANK), by_leaf(4)),
                 pl.BlockSpec((1, RANK, CHILDREN * RANK), by_leaf(3)),
+                pl.BlockSpec((1, red, red), by_leaf(3)),
+                pl.BlockSpec((1, red, RANK), by_leaf(3)),
             ),
         ),
         compiler_params=pltpu.CompilerParams(
             dimension_semantics=("arbitrary", "arbitrary"), vmem_limit_bytes=66_000_000
         ),
         name="couple",
-    )(where, leaf_nbrs, parent_nbrs, halves, shift_t2, skeleton, win_bases, win_shift)
+    )(
+        where,
+        leaf_nbrs,
+        parent_nbrs,
+        halves,
+        shift_t2,
+        skeleton,
+        *[win_bases] * group,
+        *[win_shift] * group,
+        factor,
+        panel,
+    )
 
     size = CHILDREN // per_device
     width = per_device * RANK
-    parent_block = pl.pallas_call(
+    landed = pl.pallas_call(
         functools.partial(parent_kernel, size),
-        out_shape=out((width, CHILDREN * RANK), f32),
-        grid=(1,),
-        in_specs=[
-            pl.BlockSpec((per_device, 1, RANK, CHILDREN * RANK), lambda i: (0, 0, 0, 0)),
-            vmem,
-        ],
-        out_specs=vmem,
+        out_shape=out((size, per_device, RANK, width), bf16),
+        in_specs=[anywhere],
+        out_specs=anywhere,
         scratch_shapes=[
-            pltpu.VMEM((size, per_device, RANK, width), bf16),
             pltpu.SemaphoreType.DMA((size,)),
             pltpu.SemaphoreType.DMA((size,)),
         ],
-        compiler_params=pltpu.CompilerParams(collective_id=1, has_side_effects=True),
+        compiler_params=pltpu.CompilerParams(
+            collective_id=1, has_side_effects=True, vmem_limit_bytes=66_000_000
+        ),
         name="parent",
-    )(merged, diagonal)
+    )(diagonal)
+
+    parent_block = pl.pallas_call(
+        functools.partial(symmetric_kernel, size),
+        out_shape=out((width, CHILDREN * RANK), f32),
+        grid_spec=pltpu.PrefetchScalarGridSpec(
+            num_scalar_prefetch=1,
+            grid=(size,),
+            in_specs=[
+                pl.BlockSpec((per_device, 1, RANK, width), lambda t, *_: (0, 0, 0, t)),
+                pl.BlockSpec((1, per_device, RANK, width), lambda t, *_: (t, 0, 0, 0)),
+            ],
+            out_specs=pl.BlockSpec((width, width), lambda t, *_: (0, t)),
+        ),
+        compiler_params=pltpu.CompilerParams(vmem_limit_bytes=66_000_000),
+        name="symmetric",
+    )(where, merged, landed)
     return factor, panel, merged, parent_block
 
 

time: 79.5 us -> 79.6 us (level)
  Pallas kernels: 74.1 us -> 78.2 us
  local copies, waits for them, and re-layouts: 3.63 us -> 0 us
    pallas_call x2 -> x3, Pallas kernels: 31.7 us -> 37.2 us  [the longest x1 23.2 us: local(): pl.pallas_call(functools.partial(couple_kernel, group, slots), out_shape=...]
    unnamed x7 -> x0, local copies, waits for them, and re-layouts: 3.63 us -> none
    pallas_call x1, Pallas kernels: 42.4 us -> 40.9 us  [local(): pl.pallas_call(functools.partial(window_kernel, chips, count), out_shape=...]
where the time goes in v3:
time: 79.6 us; the launch traced here: 78.8 us
  Pallas kernels  78.2 us (98%)
    pallas_call x1, Pallas kernels, local(): pl.pallas_call(functools.partial(window_kernel, chips, count), out_shape=...  40.9 us
    pallas_call x1, Pallas kernels, local(): pl.pallas_call(functools.partial(couple_kernel, group, slots), out_shape=...  23.2 us
    pallas_call x1, Pallas kernels, local(): pl.pallas_call(functools.partial(parent_kernel, size), out_shape=out((siz...  10.4 us
    pallas_call x1, Pallas kernels, local(): pl.pallas_call(functools.partial(symmetric_kernel, size), out_shape=out((...  3.7 us

profile of v3, /device:TPU:23, one launch (start us, length us, event | category | flops | bytes accessed | tf_op | source)
XLA Modules:
  0.0 78.8 jit_solution(15271194798963533225)
XLA Ops:
  0.6 40.9 %window.1 = (f32[2,128,128]{2,1,0:T(8,128)}, f32[2,128,128]{2,1,0:T(8,128)}, f32[2,128,128]{2,1,0:T(8,128)}, bf16[2,128,256]{2,1,0:T(8,128)(2,1)}, bf16[2,28,256...) custom-call(bf16[2,256,256]{2,1,0:T(8,128)(2,1)} %diag.1, ...), custom_call_target="tpu_custom_call" | custom-call | tf_op jit(solution)/shard_map/window/pallas_call | solution.py:370
  41.6 23.2 %couple.1 = (f32[2,5,128,1024]{3,2,1,0:T(8,128)}, bf16[2,128,1024]{2,1,0:T(8,128)(2,1)}, f32[2,128,128]{2,1,0:T(8,128)}, f32[2,128,128]{2,1,0:T(8,128)}) custom-call(s32[1]{0:T(128)} %bitcast.where, s32[2,26]{1,0:T(2,128)} %nbrs.1, s32[8,5]{1,0:T(8,128)} %parents.1, bf16[2,28,256,256]{3,2,1,0:T(8,128)(2,1)} %get-tuple-element.15.halves, ...), custom_call_target="tpu_custom_call" | custom-call | tf_op jit(solution)/shard_map/couple/pallas_call | solution.py:423
  64.7 10.4 %parent.1.landed = bf16[4,2,128,256]{3,2,1,0:T(8,128)(2,1)} custom-call(bf16[2,128,1024]{2,1,0:T(8,128)(2,1)} %get-tuple-element.25.diagonal), custom_call_target="tpu_custom_call" | custom-call | tf_op jit(solution)/shard_map/parent/pallas_call | solution.py:471
  75.1 3.7 %symmetric.1 = f32[256,1024]{1,0:T(8,128)} custom-call(s32[1]{0:T(128)} %bitcast.where, f32[2,5,128,1024]{3,2,1,0:T(8,128)} %get-tuple-element.13.own, bf16[4,2,128,256]{3,2,1,0:T(8,128)(2,1)} %parent.1.landed), custom_call_target="tpu_custom_call" | custom-call | tf_op jit(solution)/shard_map/symmetric/pallas_call | solution.py:486
